TPU v7x, 32 devices: a whole 2x2x4 slice. The times are simulated.
32 devices in a mesh: section: 4 (over x, core), dp: 8 (over z, y).
Axes of the slice: x: 2, y: 2, z: 4, core: 2. Of those that a mesh axis runs over, the one named last changes fastest.
Arguments:
- inputs: bfloat16 [8, 128, 8192], P(None, 'dp', 'section'), may hold values from -50 to 50
- cotangent: bfloat16 [8, 128, 8192], P(None, 'dp', 'section'), may hold values from -0.29882812 to 0.29882812
- first_factor: bfloat16 [4, 64, 128, 128], P('section'), may hold values from -0.5 to 0.5
- second_factor: bfloat16 [4, 64, 128, 128], P('section'), may hold values from -0.5 to 0.5
- gains: float32 [4, 8192], P('section'), may hold values from 0.1 to 1.9
- mixing: int32 [4, 8192], P('section'), may hold values from 0 to 8191, as said below
- order: int32 [8], replicated, may hold values from 0 to 7, each once
Outputs:
- first_grads: bfloat16 [4, 64, 128, 128], P('section')
- second_grads: bfloat16 [4, 64, 128, 128], P('section')
Inputs may be any that keep to these rules, and one draw needn't show every extreme that they name: Each row l is a stride permutation with permuted blocks and lanes: mixing[l, a*64+e] = pb[e]*128 + pa[a] for a < 128, e < 64, where pb is a permutation of 0 to 63 and pa one of 0 to 127, both drawn afresh for each layer. `order`: a permutation of 0 to 7.
All inputs are finite; a program needn't handle non-finite values.
Results may differ from a plain program's by a relative error of at most 0.015.
Values may be sent and summed in bfloat16 or wider, within the bound.
A program may use at most 64 MiB of HBM per device.

v0:
```python
import jax
import jax.numpy as jnp
from jax import lax
from jax.sharding import PartitionSpec as P

EPS = 1e-05


def shifted(x, axis, by):
    devices = lax.axis_size(axis)
    pairs = [(i, i + by) for i in range(devices) if 0 <= i + by < devices]
    return lax.ppermute(x, axis, pairs)


def block_apply(values, factor):
    row_count = values.shape[0]
    shaped = values.reshape(row_count, factor.shape[0], factor.shape[1])
    return jnp.einsum("tbi,bij->tbj", shaped, factor, preferred_element_type=jnp.float32).reshape(
        row_count, -1
    )


def block_apply_back(values, factor):
    row_count = values.shape[0]
    shaped = values.reshape(row_count, factor.shape[0], factor.shape[1])
    return jnp.einsum("tbj,bij->tbi", shaped, factor, preferred_element_type=jnp.float32).reshape(
        row_count, -1
    )


def mixing_tables(mixing_row, blocks, block_size):
    block_ids = mixing_row[:blocks] // block_size
    lane_ids = mixing_row[::blocks] % block_size
    block_table = (jnp.arange(blocks, dtype=jnp.int32)[:, None] == block_ids[None, :]).astype(
        jnp.bfloat16
    )
    lane_table = (jnp.arange(block_size, dtype=jnp.int32)[:, None] == lane_ids[None, :]).astype(
        jnp.bfloat16
    )
    return (block_table, lane_table)


def mix_forward(active, tables):
    block_table, lane_table = tables
    row_count = active.shape[0]
    shaped = active.reshape(row_count, block_table.shape[0], lane_table.shape[0])
    halfway = jnp.einsum(
        "tbi,ia->tba", shaped, lane_table, preferred_element_type=jnp.float32
    ).astype(jnp.bfloat16)
    moved = jnp.einsum(
        "tba,be->tae", halfway, block_table, preferred_element_type=jnp.float32
    ).astype(jnp.bfloat16)
    return moved.reshape(row_count, -1)


def mix_backward(grad_mixed, tables):
    block_table, lane_table = tables
    row_count = grad_mixed.shape[0]
    shaped = grad_mixed.reshape(row_count, lane_table.shape[0], block_table.shape[0])
    halfway = jnp.einsum(
        "tae,be->tab", shaped, block_table, preferred_element_type=jnp.float32
    ).astype(jnp.bfloat16)
    moved = jnp.einsum(
        "tab,ia->tbi", halfway, lane_table, preferred_element_type=jnp.float32
    ).astype(jnp.bfloat16)
    return moved.reshape(row_count, -1)


def branch_forward(hidden_in, first_block, gain_row, tables):
    as_float = hidden_in.astype(jnp.float32)
    scale_inv = lax.rsqrt(jnp.mean(as_float * as_float, axis=-1, keepdims=True) + EPS)
    unit_rows = as_float * scale_inv
    normed = (unit_rows * gain_row).astype(jnp.bfloat16)
    pre_act = block_apply(normed, first_block)
    active = (pre_act * jax.nn.sigmoid(pre_act)).astype(jnp.bfloat16)
    mixed = mix_forward(active, tables)
    return (normed, unit_rows, scale_inv, pre_act, mixed)


def layer_forward(hidden_in, first_block, second_block, gain_row, tables):
    pieces = branch_forward(hidden_in, first_block, gain_row, tables)
    return (hidden_in.astype(jnp.float32) + block_apply(pieces[4], second_block)).astype(
        jnp.bfloat16
    )


def layer_backward(hidden_in, grad_out, first_block, second_block, gain_row, tables):
    normed, unit_rows, scale_inv, pre_act, mixed = branch_forward(
        hidden_in, first_block, gain_row, tables
    )
    grad_mixed = block_apply_back(grad_out, second_block).astype(jnp.bfloat16)
    grad_active = mix_backward(grad_mixed, tables)
    gate_sig = jax.nn.sigmoid(pre_act)
    grad_pre = (
        grad_active.astype(jnp.float32) * gate_sig * (1.0 + pre_act * (1.0 - gate_sig))
    ).astype(jnp.bfloat16)
    grad_normed = block_apply_back(grad_pre, first_block)
    grad_unit = grad_normed * gain_row
    correction = jnp.mean(grad_unit * unit_rows, axis=-1, keepdims=True)
    grad_in = (
        grad_out.astype(jnp.float32) + scale_inv * (grad_unit - unit_rows * correction)
    ).astype(jnp.bfloat16)
    return (grad_in, grad_pre, normed, mixed)


def keep_slot(buffer, value, slot, is_live):
    previous = lax.dynamic_index_in_dim(buffer, slot, 0, keepdims=False)
    return lax.dynamic_update_index_in_dim(buffer, jnp.where(is_live, value, previous), slot, 0)


def body(inputs, cotangent, first_factor, second_factor, gains, mixing, order):
    sections = lax.axis_size("section")
    position = lax.axis_index("section")
    micro_count = inputs.shape[0]
    row_count = inputs.shape[1]
    whole_inputs, whole_cotangent = (
        lax.all_gather(inputs, "section", axis=2, tiled=True),
        lax.all_gather(cotangent, "section", axis=2, tiled=True),
    )
    feature_count = whole_inputs.shape[2]
    first_block = first_factor[0]
    second_block = second_factor[0]
    gain_row = gains[0]
    tables = mixing_tables(mixing[0], first_block.shape[0], first_block.shape[1])
    zero_rows = jnp.zeros((row_count, feature_count), jnp.bfloat16)
    zero_stash = jnp.zeros((micro_count, row_count, feature_count), jnp.bfloat16)
    tick_count = sections + micro_count - 1

    def forward_tick(moment, state_now):
        incoming, stashed = state_now
        slot_index = moment - position
        is_live = (slot_index >= 0) & (slot_index < micro_count)
        position_in = jnp.clip(slot_index, 0, micro_count - 1)
        entering = lax.dynamic_index_in_dim(order, position_in, 0, keepdims=False)
        fed_row = lax.dynamic_index_in_dim(whole_inputs, entering, 0, keepdims=False)
        source_rows = jnp.where(position == 0, fed_row, incoming)
        result_rows = lax.cond(
            is_live,
            lambda: layer_forward(source_rows, first_block, second_block, gain_row, tables),
            lambda: zero_rows,
        )
        stashed = keep_slot(stashed, source_rows, position_in, is_live)
        incoming = shifted(result_rows, "section", 1)
        return (incoming, stashed)

    def backward_tick(moment, state_now, stashed):
        incoming, grads_out, grads_pre, normed_keep, mixed_keep = state_now
        slot_index = moment - (sections - 1 - position)
        is_live = (slot_index >= 0) & (slot_index < micro_count)
        position_in = jnp.clip(slot_index, 0, micro_count - 1)
        given_row = lax.dynamic_index_in_dim(whole_cotangent, position_in, 0, keepdims=False)
        arriving = jnp.where(position == sections - 1, given_row, incoming)
        hidden_in = lax.dynamic_index_in_dim(stashed, position_in, 0, keepdims=False)
        grad_in, grad_pre, normed, mixed = lax.cond(
            is_live,
            lambda: layer_backward(
                hidden_in, arriving, first_block, second_block, gain_row, tables
            ),
            lambda: (zero_rows, zero_rows, zero_rows, zero_rows),
        )
        grads_out = keep_slot(grads_out, arriving, position_in, is_live)
        grads_pre = keep_slot(grads_pre, grad_pre, position_in, is_live)
        normed_keep = keep_slot(normed_keep, normed, position_in, is_live)
        mixed_keep = keep_slot(mixed_keep, mixed, position_in, is_live)
        incoming = shifted(grad_in, "section", -1)
        return (incoming, grads_out, grads_pre, normed_keep, mixed_keep)

    start_forward = (zero_rows, zero_stash)
    start_backward = (zero_rows, zero_stash, zero_stash, zero_stash, zero_stash)
    forward = lax.fori_loop(0, tick_count, forward_tick, start_forward)
    stashed = forward[1]
    backward = lax.fori_loop(
        0,
        tick_count,
        lambda moment, state_now: backward_tick(moment, state_now, stashed),
        start_backward,
    )
    blocks = first_block.shape[0]
    block_size = first_block.shape[1]
    grads_out = backward[1].reshape(-1, blocks, block_size)
    grads_pre = backward[2].reshape(-1, blocks, block_size)
    normed_all = backward[3].reshape(-1, blocks, block_size)
    mixed_all = backward[4].reshape(-1, blocks, block_size)
    part_first = jnp.einsum(
        "tbi,tbj->bij", normed_all, grads_pre, preferred_element_type=jnp.float32
    )
    part_second = jnp.einsum(
        "tbi,tbj->bij", mixed_all, grads_out, preferred_element_type=jnp.float32
    )
    summed_first, summed_second = (
        lax.psum(part_first.astype(jnp.bfloat16), "dp").astype(jnp.float32),
        lax.psum(part_second.astype(jnp.bfloat16), "dp").astype(jnp.float32),
    )
    total_first = summed_first.astype(jnp.bfloat16)
    total_second = summed_second.astype(jnp.bfloat16)
    return (total_first[None], total_second[None])


def solution(mesh):
    return jax.shard_map(
        body,
        mesh=mesh,
        in_specs=(
            P(None, "dp", "section"),
            P(None, "dp", "section"),
            P("section", None, None, None),
            P("section", None, None, None),
            P("section", None),
            P("section", None),
            P(),
        ),
        out_specs=(P("section", None, None, None), P("section", None, None, None)),
        check_vma=False,
    )
```

profile of v0, /device:TPU:24, one launch (start us, length us, event | category | flops | bytes accessed | tf_op | source)
XLA Modules:
  0.0 732.5 jit_solution(2458625787758126102)
XLA Ops:
  10.4 22.8 %all-gather.5.cloned.1.call-done = bf16[8,16,8192]{2,1,0:T(8,128)(2,1)} async-done(((bf16[8,16,2048]{2,1,0:T(8,128)(2,1)}), bf16[8,16,8192]{2,1,0:T(8,128)(2,1)}) %all-gather.5.cloned.1.call-update) | async-done | bytes 2097168 | tf_op jit(solution)/shard_map/all_gather | solution.py:117
  33.2 24.2 %all-gather.3.cloned.1.call-done = bf16[8,16,8192]{2,1,0:T(8,128)(2,1)} async-done(((bf16[8,16,2048]{2,1,0:T(8,128)(2,1)}), bf16[8,16,8192]{2,1,0:T(8,128)(2,1)}) %all-gather.3.cloned.1.call-update) | async-done | bytes 2097168 | tf_op jit(solution)/shard_map/all_gather | solution.py:118
  59.0 183.7 %while.41 = (s32[]{:T(128)}, bf16[16,8192]{1,0:T(8,128)(2,1)S(1)}, bf16[8,16,8192]{2,1,0:T(8,128)(2,1)}, s32[]{:T(128)}, pred[]{:T(512)}, /*index=5*/s32[8]{0:T(...) while((s32[]{:T(128)}, bf16[16,8192]{1,0:T(8,128)(2,1)S(1)}, ...), condition=%wide.region_4.5_spmd.clone, body=%wide.region_0.4_spmd.clone.sunk | while | flops 119971864 | bytes 12437386 | solution.py:170
  64.4 4.2 conditional.6
  77.3 4.2 conditional.6
  82.2 2.3 collective-permute-start
  91.2 4.2 conditional.6
  96.1 4.2 collective-permute-start
  106.9 4.2 conditional.6
  111.8 6.6 collective-permute-start
  125.1 4.2 conditional.6
  130.0 6.5 collective-permute-start
  143.2 4.2 conditional.6
  148.1 6.5 collective-permute-start
  161.4 4.2 conditional.6
  166.3 6.5 collective-permute-start
  179.6 4.2 conditional.6
  184.5 6.6 collective-permute-start
  198.5 10.7 %collective-permute-start = (bf16[16,8192]{1,0:T(8,128)(2,1)}, bf16[16,8192]{1,0:T(8,128)(2,1)S(1)}, u32[]{:S(2)}, u32[]{:S(2)}) collective-permute-start(bf16[16,8192]{1,0:T(8,128)(2,1)} %copy-done.6), channel_id=1, source_target_pairs={{0,8},{8,16},{16,24},{1,9},{9,17},{17,25},{2,10},{10,18},{18,26},{... | collective-permute-start | bytes 786440 | tf_op jit(solution)/shard_map/while/body/eval_jaxpr/ppermute | solution.py:12
  216.6 6.6 collective-permute-start
  230.6 10.7 %collective-permute-start = (bf16[16,8192]{1,0:T(8,128)(2,1)}, bf16[16,8192]{1,0:T(8,128)(2,1)S(1)}, u32[]{:S(2)}, u32[]{:S(2)}) collective-permute-start(bf16[16,8192]{1,0:T(8,128)(2,1)} %copy-done.6), channel_id=1, source_target_pairs={{0,8},{8,16},{16,24},{1,9},{9,17},{17,25},{2,10},{10,18},{18,26},{... | collective-permute-start | bytes 786440 | tf_op jit(solution)/shard_map/while/body/eval_jaxpr/ppermute | solution.py:12
  248.8 303.0 %while.42 = (s32[]{:T(128)}, bf16[16,8192]{1,0:T(8,128)(2,1)S(1)}, bf16[8,16,8192]{2,1,0:T(8,128)(2,1)}, bf16[8,16,8192]{2,1,0:T(8,128)(2,1)}, bf16[8,16,8192]{2...) while((s32[]{:T(128)}, bf16[16,8192]{1,0:T(8,128)(2,1)S(1)}, ...), condition=%wide.region_10.11_spmd.clone, body=%wide.region_5.10_spmd.clone.sunk | while | flops 208707616 | bytes 29847368 | solution.py:172
  251.7 2.9 conditional.7
  265.2 2.9 conditional.7
  274.1 2.6 collective-permute-done.1
  279.5 2.9 conditional.7
  288.4 35.2 %collective-permute-done.1 = bf16[16,8192]{1,0:T(8,128)(2,1)S(1)} collective-permute-done((bf16[16,8192]{1,0:T(8,128)(2,1)}, bf16[16,8192]{1,0:T(8,128)(2,1)S(1)}, u32[]{:S(2)}, u32[]{:S(2)}) %collective-permute-start.1) | collective-permute-done | bytes 262176 | tf_op jit(solution)/shard_map/while/body/eval_jaxpr/ppermute | solution.py:12
  326.4 17.2 %conditional.7 = (bf16[16,8192]{1,0:T(8,128)(2,1)}, bf16[16,8192]{1,0:T(8,128)(2,1)}, bf16[16,8192]{1,0:T(8,128)(2,1)}, bf16[16,8192]{1,0:T(8,128)(2,1)}) conditional(s32[]{:T(128)} %convert_element_type.252, () %tuple.111, (bf16[16,8192]{1,0:T(8,128)(2,1)S(1)}, bf16[8,16,8192]{2,1,0:T(8,128)(2,1)}, s32[]{:T(128)}, bf16[64,128,128]{2,1,0:T(8,128)(2,1)}, ...), branch_computations={%region_6.6_spmd, %region_7.9_spmd} | conditional | flops 208011280 | bytes 22987492 | solution.py:154
  327.5 2.8 fusion.22
  334.5 2.5 fusion.46
  339.5 2.7 fusion.31
  355.0 17.2 %conditional.7 = (bf16[16,8192]{1,0:T(8,128)(2,1)}, bf16[16,8192]{1,0:T(8,128)(2,1)}, bf16[16,8192]{1,0:T(8,128)(2,1)}, bf16[16,8192]{1,0:T(8,128)(2,1)}) conditional(s32[]{:T(128)} %convert_element_type.252, () %tuple.111, (bf16[16,8192]{1,0:T(8,128)(2,1)S(1)}, bf16[8,16,8192]{2,1,0:T(8,128)(2,1)}, s32[]{:T(128)}, bf16[64,128,128]{2,1,0:T(8,128)(2,1)}, ...), branch_computations={%region_6.6_spmd, %region_7.9_spmd} | conditional | flops 208011280 | bytes 22987492 | solution.py:154
  356.2 2.8 fusion.22
  363.2 2.5 fusion.46
  368.1 2.7 fusion.31
  383.6 17.2 %conditional.7 = (bf16[16,8192]{1,0:T(8,128)(2,1)}, bf16[16,8192]{1,0:T(8,128)(2,1)}, bf16[16,8192]{1,0:T(8,128)(2,1)}, bf16[16,8192]{1,0:T(8,128)(2,1)}) conditional(s32[]{:T(128)} %convert_element_type.252, () %tuple.111, (bf16[16,8192]{1,0:T(8,128)(2,1)S(1)}, bf16[8,16,8192]{2,1,0:T(8,128)(2,1)}, s32[]{:T(128)}, bf16[64,128,128]{2,1,0:T(8,128)(2,1)}, ...), branch_computations={%region_6.6_spmd, %region_7.9_spmd} | conditional | flops 208011280 | bytes 22987492 | solution.py:154
  384.8 2.8 fusion.22
  391.8 2.4 fusion.46
  396.7 2.7 fusion.31
  412.3 17.2 %conditional.7 = (bf16[16,8192]{1,0:T(8,128)(2,1)}, bf16[16,8192]{1,0:T(8,128)(2,1)}, bf16[16,8192]{1,0:T(8,128)(2,1)}, bf16[16,8192]{1,0:T(8,128)(2,1)}) conditional(s32[]{:T(128)} %convert_element_type.252, () %tuple.111, (bf16[16,8192]{1,0:T(8,128)(2,1)S(1)}, bf16[8,16,8192]{2,1,0:T(8,128)(2,1)}, s32[]{:T(128)}, bf16[64,128,128]{2,1,0:T(8,128)(2,1)}, ...), branch_computations={%region_6.6_spmd, %region_7.9_spmd} | conditional | flops 208011280 | bytes 22987492 | solution.py:154
  413.4 2.8 fusion.22
  420.4 2.4 fusion.46
  425.3 2.7 fusion.31
  440.9 17.2 %conditional.7 = (bf16[16,8192]{1,0:T(8,128)(2,1)}, bf16[16,8192]{1,0:T(8,128)(2,1)}, bf16[16,8192]{1,0:T(8,128)(2,1)}, bf16[16,8192]{1,0:T(8,128)(2,1)}) conditional(s32[]{:T(128)} %convert_element_type.252, () %tuple.111, (bf16[16,8192]{1,0:T(8,128)(2,1)S(1)}, bf16[8,16,8192]{2,1,0:T(8,128)(2,1)}, s32[]{:T(128)}, bf16[64,128,128]{2,1,0:T(8,128)(2,1)}, ...), branch_computations={%region_6.6_spmd, %region_7.9_spmd} | conditional | flops 208011280 | bytes 22987492 | solution.py:154
  442.0 2.8 fusion.22
  449.0 2.5 fusion.46
  453.9 2.7 fusion.31
  469.5 17.2 %conditional.7 = (bf16[16,8192]{1,0:T(8,128)(2,1)}, bf16[16,8192]{1,0:T(8,128)(2,1)}, bf16[16,8192]{1,0:T(8,128)(2,1)}, bf16[16,8192]{1,0:T(8,128)(2,1)}) conditional(s32[]{:T(128)} %convert_element_type.252, () %tuple.111, (bf16[16,8192]{1,0:T(8,128)(2,1)S(1)}, bf16[8,16,8192]{2,1,0:T(8,128)(2,1)}, s32[]{:T(128)}, bf16[64,128,128]{2,1,0:T(8,128)(2,1)}, ...), branch_computations={%region_6.6_spmd, %region_7.9_spmd} | conditional | flops 208011280 | bytes 22987492 | solution.py:154
  470.6 2.8 fusion.22
  477.6 2.4 fusion.46
  482.5 2.7 fusion.31
  498.1 17.2 %conditional.7 = (bf16[16,8192]{1,0:T(8,128)(2,1)}, bf16[16,8192]{1,0:T(8,128)(2,1)}, bf16[16,8192]{1,0:T(8,128)(2,1)}, bf16[16,8192]{1,0:T(8,128)(2,1)}) conditional(s32[]{:T(128)} %convert_element_type.252, () %tuple.111, (bf16[16,8192]{1,0:T(8,128)(2,1)S(1)}, bf16[8,16,8192]{2,1,0:T(8,128)(2,1)}, s32[]{:T(128)}, bf16[64,128,128]{2,1,0:T(8,128)(2,1)}, ...), branch_computations={%region_6.6_spmd, %region_7.9_spmd} | conditional | flops 208011280 | bytes 22987492 | solution.py:154
  499.2 2.8 fusion.22
  506.2 2.4 fusion.46
  511.1 2.7 fusion.31
  526.7 17.2 %conditional.7 = (bf16[16,8192]{1,0:T(8,128)(2,1)}, bf16[16,8192]{1,0:T(8,128)(2,1)}, bf16[16,8192]{1,0:T(8,128)(2,1)}, bf16[16,8192]{1,0:T(8,128)(2,1)}) conditional(s32[]{:T(128)} %convert_element_type.252, () %tuple.111, (bf16[16,8192]{1,0:T(8,128)(2,1)S(1)}, bf16[8,16,8192]{2,1,0:T(8,128)(2,1)}, s32[]{:T(128)}, bf16[64,128,128]{2,1,0:T(8,128)(2,1)}, ...), branch_computations={%region_6.6_spmd, %region_7.9_spmd} | conditional | flops 208011280 | bytes 22987492 | solution.py:154
  527.8 2.8 fusion.22
  534.8 2.4 fusion.46
  539.7 2.7 fusion.31
  551.8 2.3 copy.40
  558.6 4.2 convert_bitcast_fusion.2
  562.7 4.2 convert_bitcast_fusion.3
  566.9 154.4 %all-reduce.3.cloned.1.call-done = (bf16[1,64,128,128]{3,2,1,0:T(8,128)(2,1)}, bf16[1,64,128,128]{3,2,1,0:T(8,128)(2,1)}) async-done(((bf16[1,64,128,128]{3,2,1,0:T(8,128)(2,1)}, bf16[1,64,128,128]{3,2,1,0:T(8,128)(2,1)}), (bf16[1,64,128,128]{3,2,1,0:T(8,128)(2,1)}, bf16[1,64,128,128]{3,2,1,0:T(8,128)(2,1)})) %all-reduce.3.cloned.1.call-update) | async-done | bytes 4194320 | tf_op jit(solution)/shard_map/psum | solution.py:191
  721.3 3.3 copy.137
  (458 shorter events, 312.3 us)
Async XLA Ops:
  7.2 51.8 %copy-start.4 = (f32[1,8192]{1,0:T(1,128)S(1)}, f32[1,8192]{1,0:T(1,128)}, u32[]{:S(2)}) copy-start(f32[1,8192]{1,0:T(1,128)} %param.19) | copy-start | bytes 98308
  7.2 51.8 %copy-start.8 = (s32[8]{0:T(128)S(1)}, s32[8]{0:T(128)}, u32[]{:S(2)}) copy-start(s32[8]{0:T(128)} %param.21) | copy-start | bytes 100
  7.2 51.8 %copy-start = (bf16[1,64,128,128]{3,2,1,0:T(8,128)(2,1)S(1)}, bf16[1,64,128,128]{3,2,1,0:T(8,128)(2,1)}, u32[]{:S(2)}) copy-start(bf16[1,64,128,128]{3,2,1,0:T(8,128)(2,1)} %param.17) | copy-start | bytes 6291460
  7.2 26.0 %all-gather.5.cloned.1.call-start = ((), (), s32[]{:S(2)}) async-start(), calls=%async_computation.1 | async-start | bytes 2621440 | tf_op jit(solution)/shard_map/all_gather | solution.py:117
  7.9 49.4 %all-gather.3.cloned.1.call-start = ((), (), s32[]{:S(2)}) async-start(), calls=%async_computation | async-start | bytes 2621440 | tf_op jit(solution)/shard_map/all_gather | solution.py:118
  8.7 712.6 %all-reduce.3.cloned.1.call-start = ((), (), s32[]{:S(2)}) async-start(), calls=%async_computation.2 | async-start | bytes 8388608 | tf_op jit(solution)/shard_map/psum | solution.py:191
  68.6 0.7 copy-start.6
  69.3 2.6 collective-permute-start
  81.5 0.7 copy-start.6
  82.2 3.7 collective-permute-start
  95.4 0.7 copy-start.6
  96.1 5.5 collective-permute-start
  111.1 0.7 copy-start.6
  111.8 7.9 %collective-permute-start = (bf16[16,8192]{1,0:T(8,128)(2,1)}, bf16[16,8192]{1,0:T(8,128)(2,1)S(1)}, u32[]{:S(2)}, u32[]{:S(2)}) collective-permute-start(bf16[16,8192]{1,0:T(8,128)(2,1)} %copy-done.6), channel_id=1, source_target_pairs={{0,8},{8,16},{16,24},{1,9},{9,17},{17,25},{2,10},{10,18},{18,26},{... | collective-permute-start | bytes 786440 | tf_op jit(solution)/shard_map/while/body/eval_jaxpr/ppermute | solution.py:12
  129.3 0.7 copy-start.6
  130.0 7.9 %collective-permute-start = (bf16[16,8192]{1,0:T(8,128)(2,1)}, bf16[16,8192]{1,0:T(8,128)(2,1)S(1)}, u32[]{:S(2)}, u32[]{:S(2)}) collective-permute-start(bf16[16,8192]{1,0:T(8,128)(2,1)} %copy-done.6), channel_id=1, source_target_pairs={{0,8},{8,16},{16,24},{1,9},{9,17},{17,25},{2,10},{10,18},{18,26},{... | collective-permute-start | bytes 786440 | tf_op jit(solution)/shard_map/while/body/eval_jaxpr/ppermute | solution.py:12
  147.4 0.7 copy-start.6
  148.1 7.9 %collective-permute-start = (bf16[16,8192]{1,0:T(8,128)(2,1)}, bf16[16,8192]{1,0:T(8,128)(2,1)S(1)}, u32[]{:S(2)}, u32[]{:S(2)}) collective-permute-start(bf16[16,8192]{1,0:T(8,128)(2,1)} %copy-done.6), channel_id=1, source_target_pairs={{0,8},{8,16},{16,24},{1,9},{9,17},{17,25},{2,10},{10,18},{18,26},{... | collective-permute-start | bytes 786440 | tf_op jit(solution)/shard_map/while/body/eval_jaxpr/ppermute | solution.py:12
  165.6 0.7 copy-start.6
  166.3 7.8 %collective-permute-start = (bf16[16,8192]{1,0:T(8,128)(2,1)}, bf16[16,8192]{1,0:T(8,128)(2,1)S(1)}, u32[]{:S(2)}, u32[]{:S(2)}) collective-permute-start(bf16[16,8192]{1,0:T(8,128)(2,1)} %copy-done.6), channel_id=1, source_target_pairs={{0,8},{8,16},{16,24},{1,9},{9,17},{17,25},{2,10},{10,18},{18,26},{... | collective-permute-start | bytes 786440 | tf_op jit(solution)/shard_map/while/body/eval_jaxpr/ppermute | solution.py:12
  183.8 0.7 copy-start.6
  184.5 7.9 %collective-permute-start = (bf16[16,8192]{1,0:T(8,128)(2,1)}, bf16[16,8192]{1,0:T(8,128)(2,1)S(1)}, u32[]{:S(2)}, u32[]{:S(2)}) collective-permute-start(bf16[16,8192]{1,0:T(8,128)(2,1)} %copy-done.6), channel_id=1, source_target_pairs={{0,8},{8,16},{16,24},{1,9},{9,17},{17,25},{2,10},{10,18},{18,26},{... | collective-permute-start | bytes 786440 | tf_op jit(solution)/shard_map/while/body/eval_jaxpr/ppermute | solution.py:12
  197.8 0.7 copy-start.6
  198.5 12.0 %collective-permute-start = (bf16[16,8192]{1,0:T(8,128)(2,1)}, bf16[16,8192]{1,0:T(8,128)(2,1)S(1)}, u32[]{:S(2)}, u32[]{:S(2)}) collective-permute-start(bf16[16,8192]{1,0:T(8,128)(2,1)} %copy-done.6), channel_id=1, source_target_pairs={{0,8},{8,16},{16,24},{1,9},{9,17},{17,25},{2,10},{10,18},{18,26},{... | collective-permute-start | bytes 786440 | tf_op jit(solution)/shard_map/while/body/eval_jaxpr/ppermute | solution.py:12
  215.9 0.7 copy-start.6
  216.6 7.9 %collective-permute-start = (bf16[16,8192]{1,0:T(8,128)(2,1)}, bf16[16,8192]{1,0:T(8,128)(2,1)S(1)}, u32[]{:S(2)}, u32[]{:S(2)}) collective-permute-start(bf16[16,8192]{1,0:T(8,128)(2,1)} %copy-done.6), channel_id=1, source_target_pairs={{0,8},{8,16},{16,24},{1,9},{9,17},{17,25},{2,10},{10,18},{18,26},{... | collective-permute-start | bytes 786440 | tf_op jit(solution)/shard_map/while/body/eval_jaxpr/ppermute | solution.py:12
  229.9 0.7 copy-start.6
  230.6 12.1 %collective-permute-start = (bf16[16,8192]{1,0:T(8,128)(2,1)}, bf16[16,8192]{1,0:T(8,128)(2,1)S(1)}, u32[]{:S(2)}, u32[]{:S(2)}) collective-permute-start(bf16[16,8192]{1,0:T(8,128)(2,1)} %copy-done.6), channel_id=1, source_target_pairs={{0,8},{8,16},{16,24},{1,9},{9,17},{17,25},{2,10},{10,18},{18,26},{... | collective-permute-start | bytes 786440 | tf_op jit(solution)/shard_map/while/body/eval_jaxpr/ppermute | solution.py:12
  254.6 7.8 %collective-permute-start.1 = (bf16[16,8192]{1,0:T(8,128)(2,1)}, bf16[16,8192]{1,0:T(8,128)(2,1)S(1)}, u32[]{:S(2)}, u32[]{:S(2)}) collective-permute-start(bf16[16,8192]{1,0:T(8,128)(2,1)} %get-tuple-element.952), channel_id=1, source_target_pairs={{8,0},{16,8},{24,16},{9,1},{17,9},{25,17},{10,2},{18,10},{26,18},{... | collective-permute-start | bytes 786440 | tf_op jit(solution)/shard_map/while/body/eval_jaxpr/ppermute | solution.py:12
  268.1 8.5 %collective-permute-start.1 = (bf16[16,8192]{1,0:T(8,128)(2,1)}, bf16[16,8192]{1,0:T(8,128)(2,1)S(1)}, u32[]{:S(2)}, u32[]{:S(2)}) collective-permute-start(bf16[16,8192]{1,0:T(8,128)(2,1)} %get-tuple-element.952), channel_id=1, source_target_pairs={{8,0},{16,8},{24,16},{9,1},{17,9},{25,17},{10,2},{18,10},{26,18},{... | collective-permute-start | bytes 786440 | tf_op jit(solution)/shard_map/while/body/eval_jaxpr/ppermute | solution.py:12
  282.4 41.1 %collective-permute-start.1 = (bf16[16,8192]{1,0:T(8,128)(2,1)}, bf16[16,8192]{1,0:T(8,128)(2,1)S(1)}, u32[]{:S(2)}, u32[]{:S(2)}) collective-permute-start(bf16[16,8192]{1,0:T(8,128)(2,1)} %get-tuple-element.952), channel_id=1, source_target_pairs={{8,0},{16,8},{24,16},{9,1},{17,9},{25,17},{10,2},{18,10},{26,18},{... | collective-permute-start | bytes 786440 | tf_op jit(solution)/shard_map/while/body/eval_jaxpr/ppermute | solution.py:12
  337.0 2.5 copy-start.3
  339.4 2.8 copy-start.5
  343.6 8.6 %collective-permute-start.1 = (bf16[16,8192]{1,0:T(8,128)(2,1)}, bf16[16,8192]{1,0:T(8,128)(2,1)S(1)}, u32[]{:S(2)}, u32[]{:S(2)}) collective-permute-start(bf16[16,8192]{1,0:T(8,128)(2,1)} %get-tuple-element.952), channel_id=1, source_target_pairs={{8,0},{16,8},{24,16},{9,1},{17,9},{25,17},{10,2},{18,10},{26,18},{... | collective-permute-start | bytes 786440 | tf_op jit(solution)/shard_map/while/body/eval_jaxpr/ppermute | solution.py:12
  365.6 2.5 copy-start.3
  368.1 2.8 copy-start.5
  372.3 8.5 %collective-permute-start.1 = (bf16[16,8192]{1,0:T(8,128)(2,1)}, bf16[16,8192]{1,0:T(8,128)(2,1)S(1)}, u32[]{:S(2)}, u32[]{:S(2)}) collective-permute-start(bf16[16,8192]{1,0:T(8,128)(2,1)} %get-tuple-element.952), channel_id=1, source_target_pairs={{8,0},{16,8},{24,16},{9,1},{17,9},{25,17},{10,2},{18,10},{26,18},{... | collective-permute-start | bytes 786440 | tf_op jit(solution)/shard_map/while/body/eval_jaxpr/ppermute | solution.py:12
  394.2 2.5 copy-start.3
  396.7 2.8 copy-start.5
  400.9 8.6 %collective-permute-start.1 = (bf16[16,8192]{1,0:T(8,128)(2,1)}, bf16[16,8192]{1,0:T(8,128)(2,1)S(1)}, u32[]{:S(2)}, u32[]{:S(2)}) collective-permute-start(bf16[16,8192]{1,0:T(8,128)(2,1)} %get-tuple-element.952), channel_id=1, source_target_pairs={{8,0},{16,8},{24,16},{9,1},{17,9},{25,17},{10,2},{18,10},{26,18},{... | collective-permute-start | bytes 786440 | tf_op jit(solution)/shard_map/while/body/eval_jaxpr/ppermute | solution.py:12
  422.8 2.5 copy-start.3
  425.3 2.8 copy-start.5
  429.5 8.5 %collective-permute-start.1 = (bf16[16,8192]{1,0:T(8,128)(2,1)}, bf16[16,8192]{1,0:T(8,128)(2,1)S(1)}, u32[]{:S(2)}, u32[]{:S(2)}) collective-permute-start(bf16[16,8192]{1,0:T(8,128)(2,1)} %get-tuple-element.952), channel_id=1, source_target_pairs={{8,0},{16,8},{24,16},{9,1},{17,9},{25,17},{10,2},{18,10},{26,18},{... | collective-permute-start | bytes 786440 | tf_op jit(solution)/shard_map/while/body/eval_jaxpr/ppermute | solution.py:12
  451.5 2.5 copy-start.3
  453.9 2.8 copy-start.5
  458.1 8.5 %collective-permute-start.1 = (bf16[16,8192]{1,0:T(8,128)(2,1)}, bf16[16,8192]{1,0:T(8,128)(2,1)S(1)}, u32[]{:S(2)}, u32[]{:S(2)}) collective-permute-start(bf16[16,8192]{1,0:T(8,128)(2,1)} %get-tuple-element.952), channel_id=1, source_target_pairs={{8,0},{16,8},{24,16},{9,1},{17,9},{25,17},{10,2},{18,10},{26,18},{... | collective-permute-start | bytes 786440 | tf_op jit(solution)/shard_map/while/body/eval_jaxpr/ppermute | solution.py:12
  480.1 2.5 copy-start.3
  482.5 2.8 copy-start.5
  486.7 8.5 %collective-permute-start.1 = (bf16[16,8192]{1,0:T(8,128)(2,1)}, bf16[16,8192]{1,0:T(8,128)(2,1)S(1)}, u32[]{:S(2)}, u32[]{:S(2)}) collective-permute-start(bf16[16,8192]{1,0:T(8,128)(2,1)} %get-tuple-element.952), channel_id=1, source_target_pairs={{8,0},{16,8},{24,16},{9,1},{17,9},{25,17},{10,2},{18,10},{26,18},{... | collective-permute-start | bytes 786440 | tf_op jit(solution)/shard_map/while/body/eval_jaxpr/ppermute | solution.py:12
  508.7 2.5 copy-start.3
  511.1 2.8 copy-start.5
  515.3 8.5 %collective-permute-start.1 = (bf16[16,8192]{1,0:T(8,128)(2,1)}, bf16[16,8192]{1,0:T(8,128)(2,1)S(1)}, u32[]{:S(2)}, u32[]{:S(2)}) collective-permute-start(bf16[16,8192]{1,0:T(8,128)(2,1)} %get-tuple-element.952), channel_id=1, source_target_pairs={{8,0},{16,8},{24,16},{9,1},{17,9},{25,17},{10,2},{18,10},{26,18},{... | collective-permute-start | bytes 786440 | tf_op jit(solution)/shard_map/while/body/eval_jaxpr/ppermute | solution.py:12
  537.3 2.5 copy-start.3
  539.7 2.8 copy-start.5
  543.9 7.9 %collective-permute-start.1 = (bf16[16,8192]{1,0:T(8,128)(2,1)}, bf16[16,8192]{1,0:T(8,128)(2,1)S(1)}, u32[]{:S(2)}, u32[]{:S(2)}) collective-permute-start(bf16[16,8192]{1,0:T(8,128)(2,1)} %get-tuple-element.952), channel_id=1, source_target_pairs={{8,0},{16,8},{24,16},{9,1},{17,9},{25,17},{10,2},{18,10},{26,18},{... | collective-permute-start | bytes 786440 | tf_op jit(solution)/shard_map/while/body/eval_jaxpr/ppermute | solution.py:12
  551.8 2.3 copy-start.1
  554.2 1.6 copy-start.2
  721.3 3.3 copy-start.7
Sparse Core Ops, SparseCore 0:
  9.6 23.5 all-gather.4
  34.7 22.5 all-gather.2
  567.1 154.2 all-reduce.2
where the time goes:
time: 742 us; the launch traced here: 732 us
  waiting for transfers between devices  261 us (35%)
  local copies, waits for them, and re-layouts  125 us (17%)
  other arithmetic  117 us (16%)
  matrix products  110 us (15%)
  starting transfers between devices  82.6 us (11%)
  loops' own time  22.6 us (3%)
  between operations  13.8 us (2%)
    psum x1, waiting for transfers between devices, body(): lax.psum(part_first.astype(jnp.bfloat16), 'dp').astype(jnp.float32)  154 us
    ppermute x22, starting transfers between devices, shifted(): return lax.ppermute(x, axis, pairs)  82.5 us
    dynamic_update_slice x44, other arithmetic, keep_slot(): lax.dynamic_update_index_in_dim(buffer, jnp.where(is_live, value, previou...  73.7 us
    ppermute x22, waiting for transfers between devices, shifted(): return lax.ppermute(x, axis, pairs)  58.7 us
    dynamic_slice x55, local copies, waits for them, and re-layouts, keep_slot(): previous = lax.dynamic_index_in_dim(buffer, slot, 0, keepdims=False)  53.6 us
    dot_general x16, matrix products, block_apply_back(): jnp.einsum('tbj,bij->tbi', shaped, factor, preferred_element_type=jnp.flo...  40.3 us
    dot_general x24, matrix products, block_apply(): jnp.einsum('tbi,bij->tbj', shaped, factor, preferred_element_type=jnp.flo...  29.4 us
    all_gather x1, waiting for transfers between devices, body(): lax.all_gather(cotangent, 'section', axis=2, tiled=True)  24.2 us
  transfers between devices with their start and end apart: 25, of which 24 were waited for; matrix products, arithmetic and copies ran while one was open for 9% of the time, Pallas kernels for 0%

commit v1 on v0

--- a/solution.py
+++ b/solution.py
@@ -1,6 +1,10 @@
+import functools
+
 import jax
 import jax.numpy as jnp
 from jax import lax
+from jax.experimental import pallas as pl
+from jax.experimental.pallas import tpu as pltpu
 from jax.sharding import PartitionSpec as P
 
 EPS = 1e-05
@@ -196,9 +200,330 @@
     return (total_first[None], total_second[None])
 
 
+MESH = pl.DeviceIdType.MESH
+NT = (((1,), (1,)), ((), ()))
+TN = (((0,), (0,)), ((), ()))
+
+
+def rows_of(b):
+    return pl.ds(pl.multiple_of(b * 128, 128), 128)
+
+
+def step_kernel(
+    S, NB, z0, cot, w1own, w2own, gown,
+    g1, g2,
+    w1, w2, grow, gcol, z, pre, act, fstage, mixed, bstage, brecv, gbuf, gpbuf, wbuf,
+    ssend, srecv, rbuf,
+    wlocal, wsend, wrecv, fsend, frecv, bsend, brsem, sssem, srsem,
+):
+    me = lax.axis_index("section")
+    AC = 128 // S
+    D = S * NB * 128
+
+    def peer(d):
+        return lax.rem(me + d, S)
+
+    def remote(src, dst, send, recv, d):
+        return pltpu.make_async_remote_copy(
+            src_ref=src, dst_ref=dst, send_sem=send, recv_sem=recv,
+            device_id={"section": peer(d)}, device_id_type=MESH,
+        )
+
+    barrier = pltpu.get_barrier_semaphore()
+    for d in range(1, S):
+        pl.semaphore_signal(barrier, inc=1, device_id={"section": peer(d)}, device_id_type=MESH)
+    pl.semaphore_wait(barrier, S - 1)
+
+    own = ((gown, grow), (w1own, w1), (w2own, w2))
+
+    def weight_copy(k, d):
+        src, dst = own[k]
+        part = src.at[pl.ds(peer(d) * NB, NB)]
+        return remote(part, dst.at[me], wsend.at[k, d - 1], wrecv.at[k, me], d)
+
+    def weight_local(k):
+        src, dst = own[k]
+        return pltpu.make_async_copy(src.at[pl.ds(me * NB, NB)], dst.at[me], wrecv.at[k, me])
+
+    def weight_wait(k, l):
+        src, dst = own[k]
+        pltpu.make_async_copy(src.at[pl.ds(0, NB)], dst.at[l], wrecv.at[k, l]).wait()
+
+    for k in range(3):
+        for d in range(1, S):
+            weight_copy(k, d).start()
+        weight_local(k).start()
+
+    def sums_copy(k, d):
+        return remote(ssend.at[k], srecv.at[k, d - 1], sssem.at[k, d - 1], srsem.at[k, d - 1], d)
+
+    def sums_start(k, value):
+        ssend[k] = jnp.broadcast_to(value, (8, 128))
+        for d in range(1, S):
+            sums_copy(k, d).start()
+
+    def sums_wait(k):
+        for d in range(1, S):
+            sums_copy(k, d).wait()
+        total = ssend[k]
+        for d in range(1, S):
+            total = total + srecv[k, d - 1]
+        return total[0:1, :]
+
+    def fcopy(l, d):
+        return remote(
+            fstage.at[l, pl.ds(peer(d) * AC, AC)], mixed.at[l, me],
+            fsend.at[l, d - 1], frecv.at[l, d - 1], d,
+        )
+
+    def bcopy(l, d):
+        return remote(
+            bstage.at[l, peer(d)], brecv.at[l, pl.ds(me * AC, AC)],
+            bsend.at[l, d - 1], brsem.at[l, d - 1], d,
+        )
+
+    def mixed_block(l, b):
+        parts = [mixed[l, :, 2 * b + p].reshape(S * NB, 128) for p in range(2)]
+        return jnp.concatenate(parts, axis=0)
+
+    def back_send(l):
+        def block(b, carry):
+            gm = jnp.dot(w2[l, b], gbuf[rows_of(b)], preferred_element_type=jnp.float32)
+            gm = gm.astype(jnp.bfloat16)
+            for p in range(2):
+                for s in range(S):
+                    at = (p * S + s) * NB
+                    bstage[l, s, 2 * b + p] = gm[at:at + NB]
+            return carry
+        lax.fori_loop(0, NB, block, 0, unroll=UNROLL)
+        for d in range(1, S):
+            bcopy(l, d).start()
+        brecv[l, pl.ds(me * AC, AC)] = bstage[l, me]
+
+    def squares(b, total):
+        zb = z[0, rows_of(b)].astype(jnp.float32)
+        return total + jnp.sum(zb * zb, axis=0, keepdims=True)
+
+    zero = jnp.zeros((1, 128), jnp.float32)
+
+    def load_z(b, carry):
+        z[0, rows_of(b)] = z0[rows_of(b)]
+        gbuf[rows_of(b)] = cot[rows_of(b)]
+        return carry
+    lax.fori_loop(0, NB, load_z, 0)
+    sums_start(0, lax.fori_loop(0, NB, squares, zero))
+
+    for l in range(S):
+        weight_wait(0, l)
+
+    def spread(q, carry):
+        l = q // NB
+        b = lax.rem(q, NB)
+        line = jnp.broadcast_to(grow[l, pl.ds(b, 1)], (128, 128))
+        gcol[l, rows_of(b)] = line.T
+        return carry
+    lax.fori_loop(0, S * NB, spread, 0)
+
+    def forward(l, last):
+        weight_wait(1, l)
+
+        def first(b, carry):
+            zg = (z[l, rows_of(b)].astype(jnp.float32) * gcol[l, rows_of(b)]).astype(jnp.bfloat16)
+            pre[l, rows_of(b)] = lax.dot_general(
+                w1[l, b], zg, TN, preferred_element_type=jnp.float32
+            )
+            return carry
+        lax.fori_loop(0, NB, first, 0, unroll=UNROLL)
+        r = lax.rsqrt(sums_wait(l) * (1.0 / D) + EPS)
+        rbuf[l] = jnp.broadcast_to(r, (8, 128))
+
+        def gate(b, carry):
+            value = pre[l, rows_of(b)] * r
+            pre[l, rows_of(b)] = value
+            act[rows_of(b)] = value * jax.nn.sigmoid(value)
+            return carry
+        lax.fori_loop(0, NB, gate, 0, unroll=UNROLL)
+
+        def pack(a, carry):
+            fstage[l, a] = act[pl.ds(a, NB, stride=128), :].astype(jnp.bfloat16)
+            return carry
+        lax.fori_loop(0, 128, pack, 0, unroll=8)
+        for d in range(1, S):
+            fcopy(l, d).start()
+        mixed[l, me] = fstage[l, pl.ds(me * AC, AC)]
+        weight_wait(2, l)
+        if last:
+            back_send(l)
+            for d in range(1, S):
+                fcopy(l, d).wait()
+            return
+        for d in range(1, S):
+            fcopy(l, d).wait()
+
+        def second(b, total):
+            out = lax.dot_general(
+                w2[l, b], mixed_block(l, b), TN, preferred_element_type=jnp.float32
+            )
+            zn = (z[l, rows_of(b)].astype(jnp.float32) + out).astype(jnp.bfloat16)
+            z[l + 1, rows_of(b)] = zn
+            zf = zn.astype(jnp.float32)
+            return total + jnp.sum(zf * zf, axis=0, keepdims=True)
+        sums_start(l + 1, lax.fori_loop(0, NB, second, zero, unroll=UNROLL))
+
+    def backward(l, last):
+        def grad_second(b, carry):
+            g2[l, b] = lax.dot_general(
+                mixed_block(l, b), gbuf[rows_of(b)], NT, preferred_element_type=jnp.float32
+            ).astype(jnp.bfloat16)
+            return carry
+        lax.fori_loop(0, NB, grad_second, 0, unroll=UNROLL)
+        for d in range(1, S):
+            bcopy(l, d).wait()
+
+        def unpack(a, carry):
+            act[pl.ds(a, NB, stride=128), :] = brecv[l, a].astype(jnp.float32)
+            return carry
+        lax.fori_loop(0, 128, unpack, 0, unroll=8)
+        r = rbuf[l][0:1, :]
+
+        def gate(b, total):
+            value = pre[l, rows_of(b)]
+            s = jax.nn.sigmoid(value)
+            gp = (act[rows_of(b)] * s * (1.0 + value * (1.0 - s))).astype(jnp.bfloat16)
+            gpbuf[rows_of(b)] = gp
+            if last:
+                return total
+            w = jnp.dot(w1[l, b], gp, preferred_element_type=jnp.float32) * gcol[l, rows_of(b)]
+            wbuf[rows_of(b)] = w
+            u = z[l, rows_of(b)].astype(jnp.float32) * r
+            return total + jnp.sum(w * u, axis=0, keepdims=True)
+        total = lax.fori_loop(0, NB, gate, zero, unroll=UNROLL)
+        if not last:
+            sums_start(S + l, total)
+
+        def grad_first(b, carry):
+            u = z[l, rows_of(b)].astype(jnp.float32) * r
+            normed = (u * gcol[l, rows_of(b)]).astype(jnp.bfloat16)
+            g1[l, b] = lax.dot_general(
+                normed, gpbuf[rows_of(b)], NT, preferred_element_type=jnp.float32
+            ).astype(jnp.bfloat16)
+            return carry
+        lax.fori_loop(0, NB, grad_first, 0, unroll=UNROLL)
+        if last:
+            return
+        c = sums_wait(S + l) * (1.0 / D)
+
+        def grad_in(b, carry):
+            u = z[l, rows_of(b)].astype(jnp.float32) * r
+            gf = gbuf[rows_of(b)].astype(jnp.float32) + r * (wbuf[rows_of(b)] - u * c)
+            gbuf[rows_of(b)] = gf.astype(jnp.bfloat16)
+            return carry
+        lax.fori_loop(0, NB, grad_in, 0, unroll=UNROLL)
+
+    def forward_step(l, carry):
+        forward(l, False)
+        return carry
+    lax.fori_loop(0, S - 1, forward_step, 0)
+    forward(S - 1, True)
+
+    def backward_step(k, carry):
+        l = S - 1 - k
+        backward(l, False)
+        back_send(l - 1)
+        return carry
+    lax.fori_loop(0, S - 1, backward_step, 0)
+    backward(0, True)
+
+    for k in range(3):
+        for d in range(1, S):
+            weight_copy(k, d).wait_send()
+
+
+UNROLL = 4
+
+
+def local_step(S, NB, z0, cot, w1own, w2own, gown):
+    F = NB * 128
+    AC = 128 // S
+    bf, f32 = jnp.bfloat16, jnp.float32
+    vmem = pl.BlockSpec(memory_space=pltpu.VMEM)
+    dma = pltpu.SemaphoreType.DMA
+    shape = jax.ShapeDtypeStruct((S, NB, 128, 128), bf)
+    return pl.pallas_call(
+        functools.partial(step_kernel, S, NB),
+        out_shape=(shape, shape),
+        in_specs=[vmem] * 5,
+        out_specs=(vmem, vmem),
+        scratch_shapes=[
+            pltpu.VMEM((S, NB, 128, 128), bf),
+            pltpu.VMEM((S, NB, 128, 128), bf),
+            pltpu.VMEM((S, NB, 128), f32),
+            pltpu.VMEM((S, F, 128), f32),
+            pltpu.VMEM((S, F, 128), bf),
+            pltpu.VMEM((S, F, 128), f32),
+            pltpu.VMEM((F, 128), f32),
+            pltpu.VMEM((S, 128, NB, 128), bf),
+            pltpu.VMEM((S, S, AC, NB, 128), bf),
+            pltpu.VMEM((S, S, AC, NB, 128), bf),
+            pltpu.VMEM((S, 128, NB, 128), bf),
+            pltpu.VMEM((F, 128), bf),
+            pltpu.VMEM((F, 128), bf),
+            pltpu.VMEM((F, 128), f32),
+            pltpu.VMEM((2 * S, 8, 128), f32),
+            pltpu.VMEM((2 * S, S - 1, 8, 128), f32),
+            pltpu.VMEM((S, 8, 128), f32),
+            dma((1,)),
+            dma((3, S - 1)),
+            dma((3, S)),
+            dma((S, S - 1)),
+            dma((S, S - 1)),
+            dma((S, S - 1)),
+            dma((S, S - 1)),
+            dma((2 * S, S - 1)),
+            dma((2 * S, S - 1)),
+        ],
+        compiler_params=pltpu.CompilerParams(
+            collective_id=0, has_side_effects=True, vmem_limit_bytes=58 * 1024 * 1024
+        ),
+        name="step",
+    )(z0, cot, w1own, w2own, gown)
+
+
+def fast_body(inputs, cotangent, first_factor, second_factor, gains, mixing, order):
+    sections = lax.axis_size("section")
+    first_block, second_block = first_factor[0], second_factor[0]
+    blocks, size = first_block.shape[0], first_block.shape[1]
+    NB = blocks // sections
+    block_table, lane_table = mixing_tables(mixing[0], blocks, size)
+    w1p = jnp.einsum(
+        "bij,ja->bia", first_block, lane_table, preferred_element_type=jnp.float32
+    ).astype(jnp.bfloat16)
+    w2p = jnp.einsum(
+        "be,qpej->qpbj", block_table, second_block.reshape(blocks, 2, blocks, size),
+        preferred_element_type=jnp.float32,
+    ).astype(jnp.bfloat16).reshape(blocks, size, size)
+    rows = inputs.shape[0] * inputs.shape[1]
+    z0 = jnp.take(inputs, order, axis=0).reshape(rows, -1).T
+    cot = cotangent.reshape(rows, -1).T
+    g1, g2 = local_step(sections, NB, z0, cot, w1p, w2p, gains[0].reshape(blocks, size))
+    part = jnp.stack([g1, g2], axis=1)
+    part = lax.all_to_all(part, "section", split_axis=0, concat_axis=0, tiled=True)
+    total = lax.psum(part, "dp")
+    t1 = total[:, 0].reshape(blocks, size, size)
+    t2 = total[:, 1].reshape(blocks, 2, blocks, size)
+    out1 = jnp.einsum(
+        "bia,ja->bij", t1, lane_table, preferred_element_type=jnp.float32
+    ).astype(jnp.bfloat16)
+    out2 = jnp.einsum(
+        "be,qpbj->qpej", block_table, t2, preferred_element_type=jnp.float32
+    ).astype(jnp.bfloat16).reshape(blocks, size, size)
+    return (out1[None], out2[None])
+
+
 def solution(mesh):
+    quick = mesh.shape["section"] == 4
     return jax.shard_map(
-        body,
+        fast_body if quick else body,
         mesh=mesh,
         in_specs=(
             P(None, "dp", "section"),

time: 742 us -> 387 us (0.52)
  Pallas kernels: 0 us -> 139 us
  local copies, waits for them, and re-layouts: 125 us -> 8.4 us
  other arithmetic: 117 us -> 5.6 us
  waiting for transfers between devices: 261 us -> 154 us
  matrix products: 110 us -> 9.85 us
  starting transfers between devices: 82.6 us -> 0.04 us
  blocking collectives: 0 us -> 51.7 us
  loops' own time: 22.6 us -> 0 us
    pallas_call x0 -> x1, Pallas kernels: none -> 139 us  [local_step(): pl.pallas_call(functools.partial(step_kernel, S, NB), out_shape=(shape, s...]
    dot_general x66 -> x4, matrix products: 110 us -> 9.85 us  [the longest x1 3.61 us: fast_body(): jnp.einsum('bij,ja->bia', first_block, lane_table, preferred_element_type...]
    ppermute x22 -> x0, starting transfers between devices: 82.5 us -> none  [shifted(): return lax.ppermute(x, axis, pairs)]
    dynamic_update_slice x44 -> x0, other arithmetic: 73.7 us -> none  [keep_slot(): lax.dynamic_update_index_in_dim(buffer, jnp.where(is_live, value, previou...]
    dynamic_slice x66 -> x0, local copies, waits for them, and re-layouts: 60.2 us -> none  [the longest x55 53.6 us: keep_slot(): previous = lax.dynamic_index_in_dim(buffer, slot, 0, keepdims=False)]
    ppermute x22 -> x0, waiting for transfers between devices: 58.7 us -> none  [shifted(): return lax.ppermute(x, axis, pairs)]
    all_to_all x0 -> x1, blocking collectives: none -> 51.7 us  [fast_body(): lax.all_to_all(part, 'section', split_axis=0, concat_axis=0, tiled=True)]
    all_gather x2 -> x0, waiting for transfers between devices: 47 us -> none  [the longest x1 24.2 us: body(): lax.all_gather(cotangent, 'section', axis=2, tiled=True)]
  transfers between devices with their start and end apart: 25 -> 1, of which waited for: 24 -> 1; matrix products, arithmetic and copies ran while one was open for 9% -> 0% of each run, Pallas kernels for 0% -> 0%
where the time goes in v1:
time: 387 us; the launch traced here: 383 us
  waiting for transfers between devices  154 us (40%)
  Pallas kernels  139 us (36%)
  blocking collectives  51.7 us (13%)
  between operations  14.1 us (4%)
  matrix products  9.85 us (3%)
  local copies, waits for them, and re-layouts  8.4 us (2%)
  other arithmetic  5.6 us (1%)
    psum x1, waiting for transfers between devices, fast_body(): total = lax.psum(part, 'dp')  154 us
    pallas_call x1, Pallas kernels, local_step(): pl.pallas_call(functools.partial(step_kernel, S, NB), out_shape=(shape, s...  139 us
    all_to_all x1, blocking collectives, fast_body(): lax.all_to_all(part, 'section', split_axis=0, concat_axis=0, tiled=True)  51.7 us
  transfers between devices with their start and end apart: 1, of which 1 were waited for; matrix products, arithmetic and copies ran while one was open for 0% of the time, Pallas kernels for 0%

profile of v1, /device:TPU:24, one launch (start us, length us, event | category | flops | bytes accessed | tf_op | source)
XLA Modules:
  0.0 382.6 jit_solution(9988800891174482547)
XLA Ops:
  7.2 0.0 copy-start
  7.2 0.0 all-reduce.2.cloned.1.call-start
  7.2 0.8 compare_and_fusion
  8.0 0.7 compare_select_fusion
  8.7 0.7 fusion.15
  9.3 1.0 slice.13
  10.3 0.1 broadcast_in_dim.23
  10.4 0.1 broadcast_in_dim.24
  10.5 1.6 gather_fusion
  12.1 0.3 copy.19
  12.4 2.1 copy.20
  14.5 0.9 select_bitcast_fusion.z0
  15.3 3.6 convert_bitcast_fusion.1.w1own
  18.9 0.0 copy-done
  18.9 2.1 convolution_convert_fusion.1
  21.1 138.8 %step.1 = (bf16[4,16,128,128]{3,2,1,0:T(8,128)(2,1)}, bf16[4,16,128,128]{3,2,1,0:T(8,128)(2,1)}) custom-call(bf16[2048,128]{1,0:T(8,128)(2,1)} %select_bitcast_fusion.z0, bf16[2048,128]{1,0:T(8,128)(2,1)} %bitcast.48, bf16[64,128,128]{2,1,0:T(8,128)(2,1)} %convert_bitcast_fusion.1.w1own, bf16[64,128,128]{2,1,0:T(8,128)(2,1)} %bitcast.45, f32[64,128]{1,0:T(8,128)} %bitcast.54), custom_call_target="tpu_custom_call" | custom-call | tf_op jit(solution)/shard_map/step/pallas_call | solution.py:452
  159.9 2.6 pad_maximum_fusion
  162.5 0.6 copy.24
  163.1 51.7 %all_to_all.5 = bf16[4,2,16,128,128]{4,3,2,1,0:T(8,128)(2,1)} all-to-all(bf16[4,2,16,128,128]{4,3,2,1,0:T(8,128)(2,1)S(1)} %copy.24), channel_id=1, replica_groups=mesh['section'=4,'dp'=8] {'section'}, dimensions={0} | all-to-all | bytes 8388608 | tf_op jit(solution)/shard_map/all_to_all | solution.py:510
  214.9 0.0 all-reduce.2.cloned.1.call-update
  214.9 154.0 %all-reduce.2.cloned.1.call-done = bf16[4,2,16,128,128]{4,3,2,1,0:T(8,128)(2,1)} async-done(((bf16[4,2,16,128,128]{4,3,2,1,0:T(8,128)(2,1)}), bf16[4,2,16,128,128]{4,3,2,1,0:T(8,128)(2,1)}) %all-reduce.2.cloned.1.call-update) | async-done | bytes 4194320 | tf_op jit(solution)/shard_map/psum | solution.py:511
  368.9 2.7 fusion.16
  371.6 2.1 convolution_convert_fusion
  373.7 2.0 convert_bitcast_fusion
  (2 shorter events, 0.0 us)
Async XLA Ops:
  7.2 11.8 %copy-start = (bf16[1,64,128,128]{3,2,1,0:T(8,128)(2,1)S(1)}, bf16[1,64,128,128]{3,2,1,0:T(8,128)(2,1)}, u32[]{:S(2)}) copy-start(bf16[1,64,128,128]{3,2,1,0:T(8,128)(2,1)} %param.10) | copy-start | bytes 6291460
  7.2 361.7 %all-reduce.2.cloned.1.call-start = ((), (), s32[]{:S(2)}) async-start(), calls=%async_computation.1 | async-start | bytes 8388608 | tf_op jit(solution)/shard_map/psum | solution.py:511
Sparse Core Ops, SparseCore 0:
  215.0 153.8 all-reduce.1

commit v2 on v1

--- a/solution.py
+++ b/solution.py
@@ -210,29 +210,47 @@
 
 
 def step_kernel(
-    S, NB, z0, cot, w1own, w2own, gown,
-    g1, g2,
+    S, NZ, NB, z0, cot, w1own, w2own, gown,
+    out,
     w1, w2, grow, gcol, z, pre, act, fstage, mixed, bstage, brecv, gbuf, gpbuf, wbuf,
-    ssend, srecv, rbuf,
-    wlocal, wsend, wrecv, fsend, frecv, bsend, brsem, sssem, srsem,
+    ssend, srecv, rbuf, gsend, arecv, bsum, zrecv, csum, gath,
+    wsend, wrecv, fsend, frecv, bsend, brsem, sssem, srsem,
+    asend, arsem, zsend, zrsem, csend, crsem, dsend, drsem, esend, ersem, osem,
 ):
     me = lax.axis_index("section")
+    at = lax.axis_index("dp")
+    mz, my = at // 2, lax.rem(at, 2)
+    half = NB // 2
+    per = half // NZ
     AC = 128 // S
     D = S * NB * 128
 
     def peer(d):
         return lax.rem(me + d, S)
 
-    def remote(src, dst, send, recv, d):
+    def z_at(d):
+        return lax.rem(mz + d, NZ)
+
+    def z_peer(d):
+        return {"dp": z_at(d) * 2 + my}
+
+    def remote_to(src, dst, send, recv, device):
         return pltpu.make_async_remote_copy(
             src_ref=src, dst_ref=dst, send_sem=send, recv_sem=recv,
-            device_id={"section": peer(d)}, device_id_type=MESH,
-        )
+            device_id=device, device_id_type=MESH,
+        )
+
+    def remote(src, dst, send, recv, d):
+        return remote_to(src, dst, send, recv, {"section": peer(d)})
 
     barrier = pltpu.get_barrier_semaphore()
     for d in range(1, S):
         pl.semaphore_signal(barrier, inc=1, device_id={"section": peer(d)}, device_id_type=MESH)
-    pl.semaphore_wait(barrier, S - 1)
+    y_peer = {"dp": mz * 2 + 1 - my}
+    pl.semaphore_signal(barrier, inc=1, device_id=y_peer, device_id_type=MESH)
+    for d in range(1, NZ):
+        pl.semaphore_signal(barrier, inc=1, device_id=z_peer(d), device_id_type=MESH)
+    pl.semaphore_wait(barrier, S + NZ - 1)
 
     own = ((gown, grow), (w1own, w1), (w2own, w2))
 
@@ -370,13 +388,95 @@
             return total + jnp.sum(zf * zf, axis=0, keepdims=True)
         sums_start(l + 1, lax.fori_loop(0, NB, second, zero, unroll=UNROLL))
 
+    def a_copy(l, f):
+        return remote_to(
+            gsend.at[l, f, 1 - my], arecv.at[l, f], asend.at[l, f], arsem.at[l, f], y_peer
+        )
+
+    def b_copy(l, f, d):
+        return remote_to(
+            bsum.at[l, f, pl.ds(z_at(d) * per, per)], zrecv.at[l, f, d - 1],
+            zsend.at[l, f, d - 1], zrsem.at[l, f, d - 1], z_peer(d),
+        )
+
+    def c_copy(l, f):
+        return remote_to(
+            csum.at[l, f], gath.at[f, me, my, mz], csend.at[l, f], crsem.at[f, me], {"section": l}
+        )
+
+    def d_copy(f, d):
+        part = gath.at[f, :, my, mz]
+        return remote_to(part, part, dsend.at[f, d - 1], drsem.at[f, d - 1], z_peer(d))
+
+    def e_copy(f, d):
+        part = gath.at[f, :, my, lax.rem(mz + NZ - d, NZ)]
+        return remote_to(part, part, esend.at[f, d], ersem.at[f, d], y_peer)
+
+    def stage_b(l, f):
+        a_copy(l, f).wait_recv()
+
+        def tile(i, carry):
+            total = gsend[l, f, my, i].astype(jnp.float32) + arecv[l, f, i].astype(jnp.float32)
+            bsum[l, f, i] = total.astype(jnp.bfloat16)
+            return carry
+        lax.fori_loop(0, half, tile, 0)
+        for d in range(1, NZ):
+            b_copy(l, f, d).start()
+
+    def stage_c(l, f):
+        for d in range(1, NZ):
+            b_copy(l, f, d).wait_recv()
+        for i in range(per):
+            total = bsum[l, f, mz * per + i].astype(jnp.float32)
+            for d in range(1, NZ):
+                total = total + zrecv[l, f, d - 1, i].astype(jnp.float32)
+            csum[l, f, i] = total.astype(jnp.bfloat16)
+
+        @pl.when(me == l)
+        def _():
+            gath[f, me, my, mz] = csum[l, f]
+
+        @pl.when(me != l)
+        def _():
+            c_copy(l, f).start()
+
+    def stage_d(l, f):
+        @pl.when(me == l)
+        def _():
+            for d in range(1, S):
+                part = gath.at[f, peer(d), my, mz]
+                pltpu.make_async_copy(csum.at[l, f], part, crsem.at[f, peer(d)]).wait()
+            for d in range(1, NZ):
+                d_copy(f, d).start()
+            e_copy(f, 0).start()
+
+    def stage_e(l, f):
+        @pl.when(me == l)
+        def _():
+            for d in range(1, NZ):
+                d_copy(f, d).wait_recv()
+                e_copy(f, d).start()
+
+    def both(stage, l):
+        for f in (1, 0):
+            stage(l, f)
+
     def backward(l, last):
         def grad_second(b, carry):
-            g2[l, b] = lax.dot_general(
+            gsend[l, 1, b // half, lax.rem(b, half)] = lax.dot_general(
                 mixed_block(l, b), gbuf[rows_of(b)], NT, preferred_element_type=jnp.float32
             ).astype(jnp.bfloat16)
             return carry
         lax.fori_loop(0, NB, grad_second, 0, unroll=UNROLL)
+        a_copy(l, 1).start()
+
+        @pl.when(l < S - 1)
+        def _():
+            both(stage_b, l + 1)
+
+        @pl.when(l < S - 2)
+        def _():
+            both(stage_d, l + 2)
         for d in range(1, S):
             bcopy(l, d).wait()
 
@@ -404,11 +504,20 @@
         def grad_first(b, carry):
             u = z[l, rows_of(b)].astype(jnp.float32) * r
             normed = (u * gcol[l, rows_of(b)]).astype(jnp.bfloat16)
-            g1[l, b] = lax.dot_general(
+            gsend[l, 0, b // half, lax.rem(b, half)] = lax.dot_general(
                 normed, gpbuf[rows_of(b)], NT, preferred_element_type=jnp.float32
             ).astype(jnp.bfloat16)
             return carry
         lax.fori_loop(0, NB, grad_first, 0, unroll=UNROLL)
+        a_copy(l, 0).start()
+
+        @pl.when(l < S - 1)
+        def _():
+            both(stage_c, l + 1)
+
+        @pl.when(l < S - 2)
+        def _():
+            both(stage_e, l + 2)
         if last:
             return
         c = sums_wait(S + l) * (1.0 / D)
@@ -433,6 +542,36 @@
         return carry
     lax.fori_loop(0, S - 1, backward_step, 0)
     backward(0, True)
+    stage_b(0, 1)
+    both(stage_d, 1)
+    stage_b(0, 0)
+    both(stage_e, 1)
+    both(stage_c, 0)
+    both(stage_d, 0)
+    both(stage_e, 0)
+    for f in range(2):
+        for d in range(NZ):
+            e_copy(f, d).wait_recv()
+    done = pltpu.make_async_copy(gath, out, osem.at[0])
+    done.start()
+
+    def finish(l, carry):
+        for f in range(2):
+            a_copy(l, f).wait_send()
+            for d in range(1, NZ):
+                b_copy(l, f, d).wait_send()
+
+            @pl.when(me != l)
+            def _():
+                c_copy(l, f).wait_send()
+        return carry
+    lax.fori_loop(0, S, finish, 0)
+    for f in range(2):
+        for d in range(1, NZ):
+            d_copy(f, d).wait_send()
+        for d in range(NZ):
+            e_copy(f, d).wait_send()
+    done.wait()
 
     for k in range(3):
         for d in range(1, S):
@@ -442,18 +581,20 @@
 UNROLL = 4
 
 
-def local_step(S, NB, z0, cot, w1own, w2own, gown):
+def local_step(S, NZ, NB, z0, cot, w1own, w2own, gown):
     F = NB * 128
     AC = 128 // S
     bf, f32 = jnp.bfloat16, jnp.float32
     vmem = pl.BlockSpec(memory_space=pltpu.VMEM)
     dma = pltpu.SemaphoreType.DMA
-    shape = jax.ShapeDtypeStruct((S, NB, 128, 128), bf)
+    half = NB // 2
+    per = half // NZ
+    shape = jax.ShapeDtypeStruct((2, S, 2, NZ, per, 128, 128), bf)
     return pl.pallas_call(
-        functools.partial(step_kernel, S, NB),
-        out_shape=(shape, shape),
+        functools.partial(step_kernel, S, NZ, NB),
+        out_shape=shape,
         in_specs=[vmem] * 5,
-        out_specs=(vmem, vmem),
+        out_specs=pl.BlockSpec(memory_space=pl.ANY),
         scratch_shapes=[
             pltpu.VMEM((S, NB, 128, 128), bf),
             pltpu.VMEM((S, NB, 128, 128), bf),
@@ -472,7 +613,12 @@
             pltpu.VMEM((2 * S, 8, 128), f32),
             pltpu.VMEM((2 * S, S - 1, 8, 128), f32),
             pltpu.VMEM((S, 8, 128), f32),
-            dma((1,)),
+            pltpu.VMEM((S, 2, 2, half, 128, 128), bf),
+            pltpu.VMEM((S, 2, half, 128, 128), bf),
+            pltpu.VMEM((S, 2, half, 128, 128), bf),
+            pltpu.VMEM((S, 2, NZ - 1, per, 128, 128), bf),
+            pltpu.VMEM((S, 2, per, 128, 128), bf),
+            pltpu.VMEM((2, S, 2, NZ, per, 128, 128), bf),
             dma((3, S - 1)),
             dma((3, S)),
             dma((S, S - 1)),
@@ -481,6 +627,17 @@
             dma((S, S - 1)),
             dma((2 * S, S - 1)),
             dma((2 * S, S - 1)),
+            dma((S, 2)),
+            dma((S, 2)),
+            dma((S, 2, NZ - 1)),
+            dma((S, 2, NZ - 1)),
+            dma((S, 2)),
+            dma((2, S)),
+            dma((2, NZ - 1)),
+            dma((2, NZ - 1)),
+            dma((2, NZ)),
+            dma((2, NZ)),
+            dma((1,)),
         ],
         compiler_params=pltpu.CompilerParams(
             collective_id=0, has_side_effects=True, vmem_limit_bytes=58 * 1024 * 1024
@@ -505,12 +662,11 @@
     rows = inputs.shape[0] * inputs.shape[1]
     z0 = jnp.take(inputs, order, axis=0).reshape(rows, -1).T
     cot = cotangent.reshape(rows, -1).T
-    g1, g2 = local_step(sections, NB, z0, cot, w1p, w2p, gains[0].reshape(blocks, size))
-    part = jnp.stack([g1, g2], axis=1)
-    part = lax.all_to_all(part, "section", split_axis=0, concat_axis=0, tiled=True)
-    total = lax.psum(part, "dp")
-    t1 = total[:, 0].reshape(blocks, size, size)
-    t2 = total[:, 1].reshape(blocks, 2, blocks, size)
+    total = local_step(
+        sections, lax.axis_size("dp") // 2, NB, z0, cot, w1p, w2p, gains[0].reshape(blocks, size)
+    )
+    t1 = total[0].reshape(blocks, size, size)
+    t2 = total[1].reshape(blocks, 2, blocks, size)
     out1 = jnp.einsum(
         "bia,ja->bij", t1, lane_table, preferred_element_type=jnp.float32
     ).astype(jnp.bfloat16)
@@ -521,7 +677,7 @@
 
 
 def solution(mesh):
-    quick = mesh.shape["section"] == 4
+    quick = mesh.shape["section"] == 4 and mesh.shape["dp"] == 8
     return jax.shard_map(
         fast_body if quick else body,
         mesh=mesh,

time: 387 us -> 282 us (0.73); the launches traced: 383 us -> 282 us
  waiting for transfers between devices: 154 us -> 0 us
  Pallas kernels: 139 us -> 259 us
  blocking collectives: 51.7 us -> 0 us
  between operations: 14.1 us -> 0.68 us
    psum x1 -> x0, waiting for transfers between devices: 154 us -> none  [fast_body(): total = lax.psum(part, 'dp')]
    pallas_call x1, Pallas kernels: 139 us -> 259 us  [local_step(): pl.pallas_call(functools.partial(step_kernel, S, NZ, NB), out_shape=shape...]
    all_to_all x1 -> x0, blocking collectives: 51.7 us -> none  [fast_body(): lax.all_to_all(part, 'section', split_axis=0, concat_axis=0, tiled=True)]
  transfers between devices with their start and end apart: 1 -> 0, of which waited for: 1 -> 0; matrix products, arithmetic and copies ran while one was open for 0% -> 0% of each run, Pallas kernels for 0% -> 0%
where the time goes in v2:
time: 282 us
  Pallas kernels  259 us (92%)
  matrix products  9.84 us (3%)
  local copies, waits for them, and re-layouts  9.39 us (3%)
  other arithmetic  2.86 us (1%)
    pallas_call x1, Pallas kernels, local_step(): pl.pallas_call(functools.partial(step_kernel, S, NZ, NB), out_shape=shape...  259 us

profile of v2, /device:TPU:24, one launch (start us, length us, event | category | flops | bytes accessed | tf_op | source)
XLA Modules:
  0.0 281.5 jit_solution(17610471192585457495)
XLA Ops:
  0.6 0.0 copy-start
  0.6 1.6 copy-done
  2.2 0.7 fusion.15
  2.9 1.0 slice.13
  3.9 0.7 compare_and_fusion
  4.5 0.1 broadcast_in_dim.23
  4.6 0.1 broadcast_in_dim.24
  4.7 0.7 compare_select_fusion
  5.4 1.6 gather_fusion
  7.0 0.3 copy.14
  7.3 0.8 select_bitcast_fusion.z0
  8.1 2.1 copy.15
  10.2 3.6 %convert_bitcast_fusion.1.w1own = bf16[64,128,128]{2,1,0:T(8,128)(2,1)} fusion(bf16[1,64,128,128]{3,2,1,0:T(8,128)(2,1)} %param.9, s32[128]{0:T(128)S(1)} %and_select_fusion.1), kind=kOutput, calls=%fused_computation.4 | convolution fusion | flops 269500416 | bytes 4194816 | tf_op jit(solution)/shard_map/bij,ja->bia/dot_general | solution.py:655
  13.8 2.1 convolution_convert_fusion.1
  15.9 258.8 %step.1 = bf16[2,4,2,4,2,128,128]{6,5,4,3,2,1,0:T(8,128)(2,1)} custom-call(bf16[2048,128]{1,0:T(8,128)(2,1)} %select_bitcast_fusion.z0, bf16[2048,128]{1,0:T(8,128)(2,1)} %bitcast.46, bf16[64,128,128]{2,1,0:T(8,128)(2,1)} %convert_bitcast_fusion.1.w1own, bf16[64,128,128]{2,1,0:T(8,128)(2,1)} %bitcast.45, f32[64,128]{1,0:T(8,128)} %bitcast.50), custom_call_target="tpu_custom_call" | custom-call | tf_op jit(solution)/shard_map/step/pallas_call | solution.py:593
  274.7 2.7 fusion.16
  277.4 2.1 convolution_convert_fusion
  279.5 2.0 convert_bitcast_fusion
  (2 shorter events, 0.0 us)
Async XLA Ops:
  0.6 1.6 copy-start

commit v3 on v2

--- a/solution.py
+++ b/solution.py
@@ -267,10 +267,16 @@
         src, dst = own[k]
         pltpu.make_async_copy(src.at[pl.ds(0, NB)], dst.at[l], wrecv.at[k, l]).wait()
 
+    even = lax.rem(me, 2) == 0
     for k in range(3):
+        weight_local(k).start()
+    for d in range(1, S):
+        weight_copy(0, d).start()
+
+    @pl.when(even)
+    def _():
         for d in range(1, S):
-            weight_copy(k, d).start()
-        weight_local(k).start()
+            weight_copy(1, d).start()
 
     def sums_copy(k, d):
         return remote(ssend.at[k], srecv.at[k, d - 1], sssem.at[k, d - 1], srsem.at[k, d - 1], d)
@@ -343,6 +349,20 @@
     lax.fori_loop(0, S * NB, spread, 0)
 
     def forward(l, last):
+        if not last:
+            @pl.when((l == 0) & even)
+            def _():
+                for d in range(1, S):
+                    weight_copy(1, d).wait_send()
+                for d in range(2, S):
+                    weight_copy(2, d).start()
+
+            @pl.when((l == 1) & jnp.logical_not(even))
+            def _():
+                for d in range(1, S):
+                    weight_copy(1, d).wait_send()
+                for d in range(1, S):
+                    weight_copy(2, d).start()
         weight_wait(1, l)
 
         def first(b, carry):
@@ -369,7 +389,18 @@
         for d in range(1, S):
             fcopy(l, d).start()
         mixed[l, me] = fstage[l, pl.ds(me * AC, AC)]
+        if not last:
+            @pl.when((l == 0) & even)
+            def _():
+                for d in range(2, S):
+                    weight_copy(2, d).wait_send()
+                weight_copy(2, 1).start()
         weight_wait(2, l)
+        if not last:
+            @pl.when((l == 0) & jnp.logical_not(even))
+            def _():
+                for d in range(1, S):
+                    weight_copy(1, d).start()
         if last:
             back_send(l)
             for d in range(1, S):
@@ -472,11 +503,12 @@
 
         @pl.when(l < S - 1)
         def _():
-            both(stage_b, l + 1)
+            stage_b(l + 1, 0)
 
         @pl.when(l < S - 2)
         def _():
-            both(stage_d, l + 2)
+            stage_c(l + 2, 0)
+            stage_d(l + 2, 1)
         for d in range(1, S):
             bcopy(l, d).wait()
 
@@ -511,13 +543,15 @@
         lax.fori_loop(0, NB, grad_first, 0, unroll=UNROLL)
         a_copy(l, 0).start()
 
+        stage_b(l, 1)
+
         @pl.when(l < S - 1)
         def _():
-            both(stage_c, l + 1)
+            stage_c(l + 1, 1)
 
         @pl.when(l < S - 2)
         def _():
-            both(stage_e, l + 2)
+            stage_d(l + 2, 0)
         if last:
             return
         c = sums_wait(S + l) * (1.0 / D)
@@ -542,13 +576,20 @@
         return carry
     lax.fori_loop(0, S - 1, backward_step, 0)
     backward(0, True)
-    stage_b(0, 1)
-    both(stage_d, 1)
+    stage_d(1, 1)
     stage_b(0, 0)
-    both(stage_e, 1)
-    both(stage_c, 0)
-    both(stage_d, 0)
-    both(stage_e, 0)
+    stage_c(1, 0)
+    stage_c(0, 1)
+    for l in range(S - 1, 1, -1):
+        both(stage_e, l)
+    stage_e(1, 1)
+    stage_d(1, 0)
+    stage_c(0, 0)
+    stage_d(0, 1)
+    stage_e(1, 0)
+    stage_e(0, 1)
+    stage_d(0, 0)
+    stage_e(0, 0)
     for f in range(2):
         for d in range(NZ):
             e_copy(f, d).wait_recv()
@@ -573,9 +614,14 @@
             e_copy(f, d).wait_send()
     done.wait()
 
-    for k in range(3):
-        for d in range(1, S):
-            weight_copy(k, d).wait_send()
+    for d in range(1, S):
+        weight_copy(0, d).wait_send()
+    weight_copy(2, 1).wait_send()
+
+    @pl.when(jnp.logical_not(even))
+    def _():
+        for d in range(2, S):
+            weight_copy(2, d).wait_send()
 
 
 UNROLL = 4

time: 282 us -> 261 us (0.926)
  Pallas kernels: 259 us -> 238 us
    pallas_call x1, Pallas kernels: 259 us -> 238 us  [local_step(): pl.pallas_call(functools.partial(step_kernel, S, NZ, NB), out_shape=shape...]
where the time goes in v3:
time: 261 us
  Pallas kernels  238 us (91%)
  matrix products  9.86 us (4%)
  local copies, waits for them, and re-layouts  9.39 us (4%)
  other arithmetic  2.86 us (1%)
    pallas_call x1, Pallas kernels, local_step(): pl.pallas_call(functools.partial(step_kernel, S, NZ, NB), out_shape=shape...  238 us

profile of v3, /device:TPU:24, one launch (start us, length us, event | category | flops | bytes accessed | tf_op | source)
XLA Modules:
  0.0 260.7 jit_solution(14569374957423326721)
XLA Ops:
  0.6 0.0 copy-start
  0.6 1.6 copy-done
  2.2 0.7 fusion.15
  2.9 1.0 slice.13
  3.9 0.7 compare_and_fusion
  4.5 0.1 broadcast_in_dim.23
  4.6 0.1 broadcast_in_dim.24
  4.7 0.7 compare_select_fusion
  5.4 1.6 gather_fusion
  7.0 0.3 copy.14
  7.3 0.8 select_bitcast_fusion.z0
  8.1 2.1 copy.15
  10.2 3.6 %convert_bitcast_fusion.1.w1own = bf16[64,128,128]{2,1,0:T(8,128)(2,1)} fusion(bf16[1,64,128,128]{3,2,1,0:T(8,128)(2,1)} %param.9, s32[128]{0:T(128)S(1)} %and_select_fusion.1), kind=kOutput, calls=%fused_computation.4 | convolution fusion | flops 269500416 | bytes 4194816 | tf_op jit(solution)/shard_map/bij,ja->bia/dot_general | solution.py:701
  13.8 2.1 convolution_convert_fusion.1
  15.9 237.9 %step.1 = bf16[2,4,2,4,2,128,128]{6,5,4,3,2,1,0:T(8,128)(2,1)} custom-call(bf16[2048,128]{1,0:T(8,128)(2,1)} %select_bitcast_fusion.z0, bf16[2048,128]{1,0:T(8,128)(2,1)} %bitcast.46, bf16[64,128,128]{2,1,0:T(8,128)(2,1)} %convert_bitcast_fusion.1.w1own, bf16[64,128,128]{2,1,0:T(8,128)(2,1)} %bitcast.45, f32[64,128]{1,0:T(8,128)} %bitcast.50), custom_call_target="tpu_custom_call" | custom-call | tf_op jit(solution)/shard_map/step/pallas_call | solution.py:639
  253.8 2.7 %fusion.16 = (bf16[1,4,2,4,2,128,128]{6,5,4,3,2,1,0:T(8,128)(2,1)S(1)}, bf16[1,4,2,4,2,128,128]{6,5,4,3,2,1,0:T(8,128)(2,1)S(1)}) fusion(bf16[2,4,2,4,2,128,128]{6,5,4,3,2,1,0:T(8,128)(2,1)} %step.1), kind=kLoop, calls=%fused_computation.28 | loop fusion | bytes 8388608 | tf_op jit(solution)/shard_map/slice | solution.py:715
  256.6 2.1 convolution_convert_fusion
  258.6 2.0 convert_bitcast_fusion
  (2 shorter events, 0.0 us)
Async XLA Ops:
  0.6 1.6 copy-start

commit v4 on v3

--- a/solution.py
+++ b/solution.py
@@ -624,7 +624,7 @@
             weight_copy(2, d).wait_send()
 
 
-UNROLL = 4
+UNROLL = 8
 
 
 def local_step(S, NZ, NB, z0, cot, w1own, w2own, gown):

time: 261 us -> 259 us (level)
  no operation moved by 1% of the time
where the time goes in v4:
time: 259 us
  Pallas kernels  236 us (91%)
  matrix products  9.84 us (4%)
  local copies, waits for them, and re-layouts  9.39 us (4%)
  other arithmetic  2.86 us (1%)
    pallas_call x1, Pallas kernels, local_step(): pl.pallas_call(functools.partial(step_kernel, S, NZ, NB), out_shape=shape...  236 us

profile of v4, /device:TPU:24, one launch (start us, length us, event | category | flops | bytes accessed | tf_op | source)
XLA Modules:
  0.0 258.7 jit_solution(16059682309367652868)
XLA Ops:
  0.6 0.0 copy-start
  0.6 1.6 copy-done
  2.2 0.7 fusion.15
  2.9 1.0 slice.13
  3.9 0.7 compare_and_fusion
  4.5 0.1 broadcast_in_dim.23
  4.6 0.1 broadcast_in_dim.24
  4.7 0.7 compare_select_fusion
  5.4 1.6 gather_fusion
  7.0 0.3 copy.14
  7.3 0.8 select_bitcast_fusion.z0
  8.1 2.1 copy.15
  10.2 3.6 %convert_bitcast_fusion.1.w1own = bf16[64,128,128]{2,1,0:T(8,128)(2,1)} fusion(bf16[1,64,128,128]{3,2,1,0:T(8,128)(2,1)} %param.9, s32[128]{0:T(128)S(1)} %and_select_fusion.1), kind=kOutput, calls=%fused_computation.4 | convolution fusion | flops 269500416 | bytes 4194816 | tf_op jit(solution)/shard_map/bij,ja->bia/dot_general | solution.py:701
  13.8 2.1 convolution_convert_fusion.1
  15.9 235.9 %step.1 = bf16[2,4,2,4,2,128,128]{6,5,4,3,2,1,0:T(8,128)(2,1)} custom-call(bf16[2048,128]{1,0:T(8,128)(2,1)} %select_bitcast_fusion.z0, bf16[2048,128]{1,0:T(8,128)(2,1)} %bitcast.46, bf16[64,128,128]{2,1,0:T(8,128)(2,1)} %convert_bitcast_fusion.1.w1own, bf16[64,128,128]{2,1,0:T(8,128)(2,1)} %bitcast.45, f32[64,128]{1,0:T(8,128)} %bitcast.50), custom_call_target="tpu_custom_call" | custom-call | tf_op jit(solution)/shard_map/step/pallas_call | solution.py:639
  251.9 2.7 %fusion.16 = (bf16[1,4,2,4,2,128,128]{6,5,4,3,2,1,0:T(8,128)(2,1)S(1)}, bf16[1,4,2,4,2,128,128]{6,5,4,3,2,1,0:T(8,128)(2,1)S(1)}) fusion(bf16[2,4,2,4,2,128,128]{6,5,4,3,2,1,0:T(8,128)(2,1)} %step.1), kind=kLoop, calls=%fused_computation.28 | loop fusion | bytes 8388608 | tf_op jit(solution)/shard_map/slice | solution.py:715
  254.6 2.1 convolution_convert_fusion
  256.7 2.0 convert_bitcast_fusion
  (2 shorter events, 0.0 us)
Async XLA Ops:
  0.6 1.6 copy-start
